TPU v7x, 128 devices: a whole 4x4x4 slice. The times are simulated.
128 devices in a mesh: group: 8 (over z, core), patch: 16 (over x, y).
Axes of the slice: x: 4, y: 4, z: 4, core: 2. Of those that a mesh axis runs over, the one named last changes fastest.
Arguments:
- node_latent: bfloat16 [40960, 512], P(('group', 'patch')), may hold values from -6 to 6
- fine_latent: bfloat16 [262144, 512], P(('group', 'patch')), may hold values from -6 to 6
- coarse_latent: bfloat16 [65536, 512], P(('group', 'patch')), may hold values from -6 to 6
- fine_sender: int32 [262144], P(('group', 'patch')), may hold values from 0 to 447
- fine_receiver: int32 [262144], P(('group', 'patch')), may hold values from 0 to 319
- coarse_owner: int32 [65536, 1], P(('group', 'patch')), may hold values from 0 to 127; in each aligned block of 512 rows (0 to 511, 512 to 1023, ...) at most 8 rows name the same one
- coarse_row: int32 [65536], P(('group', 'patch')), may hold values from 0 to 15
- coarse_receiver: int32 [65536], P(('group', 'patch')), may hold values from 0 to 15
- edge_first: bfloat16 [2, 1536, 512], replicated, may hold values from -0.15625 to 0.15625
- edge_bias: float32 [2, 512], replicated, may hold values from -3 to 3
- edge_second: bfloat16 [2, 512, 512], replicated, may hold values from -0.25 to 0.25
- edge_gain: float32 [2, 512], replicated, may hold values from 0.25 to 1.75
- node_first: bfloat16 [2, 1024, 512], replicated, may hold values from -0.1875 to 0.1875
- node_bias: float32 [2, 512], replicated, may hold values from -3 to 3
- node_second: bfloat16 [2, 512, 512], replicated, may hold values from -0.25 to 0.25
- node_gain: float32 [2, 512], replicated, may hold values from 0.25 to 1.75
Outputs:
- node_out: bfloat16 [40960, 512], P(('group', 'patch'))
- fine_out: bfloat16 [262144, 512], P(('group', 'patch'))
- coarse_out: bfloat16 [65536, 512], P(('group', 'patch'))
Inputs may be any that keep to these rules, and one draw needn't show every extreme that they name: `fine_sender`: A fine edge's sender indexes the receiving device's patch extended by 64 nodes on each side: values below 64 are the last 64 nodes of the previous patch of the same group, values from 384 on the first 64 nodes of the next patch; patches of a group close into a loop. `coarse_owner`: among the 512 coarse edges of one device, at most 8 have their sender on any one device.
All inputs are finite; a program needn't handle non-finite values.
Results may differ from a plain program's by a relative error of at most 0.0095.
Values may be sent and summed in bfloat16 or wider, within the bound.
A program may use at most 128 MiB of HBM per device.

v0:
```python
import jax
import jax.numpy as jnp
from jax import lax
from jax.sharding import PartitionSpec as P

HALO = 64
COARSE = 16
LAYERS = 2
EPSILON = 1e-05


def padded_2(block, sides, width):
    for axis, dim in sides:
        count = lax.axis_size(axis)
        forward = [(i, i + 1) for i in range(count - 1)]
        forward.append((count - 1, 0))
        backward = [(target, source) for source, target in forward]
        low = lax.ppermute(
            lax.slice_in_dim(block, block.shape[dim] - width, None, axis=dim), axis, forward
        )
        high = lax.ppermute(lax.slice_in_dim(block, 0, width, axis=dim), axis, backward)
        block = jnp.concatenate([low, block, high], axis=dim)
    return block


def norm_rows(values, gain_row):
    centre = jnp.mean(values, axis=-1, keepdims=True)
    centred = values - centre
    variance = jnp.mean(centred * centred, axis=-1, keepdims=True)
    return centred * lax.rsqrt(variance + EPSILON) * gain_row


def select_rows(selector, table):
    return jnp.dot(selector, table, preferred_element_type=jnp.float32).astype(jnp.bfloat16)


def edge_block(latent, endpoints, weight_edge, weight_pair, bias_row, weight_second, gain_row):
    from_ends = jnp.dot(endpoints, weight_pair, preferred_element_type=jnp.float32)
    pre = jnp.dot(latent, weight_edge, preferred_element_type=jnp.float32) + from_ends + bias_row
    hidden = jax.nn.silu(pre).astype(jnp.bfloat16)
    output = jnp.dot(hidden, weight_second, preferred_element_type=jnp.float32)
    message = norm_rows(output, gain_row)
    updated = (latent.astype(jnp.float32) + message).astype(jnp.bfloat16)
    return (updated, message.astype(jnp.bfloat16))


def body(
    node_latent,
    fine_latent,
    coarse_latent,
    fine_sender,
    fine_receiver,
    coarse_owner,
    coarse_row,
    coarse_receiver,
    edge_first,
    edge_bias,
    edge_second,
    edge_gain,
    node_first,
    node_bias,
    node_second,
    node_gain,
):
    width = node_latent.shape[1]
    node_count = node_latent.shape[0]
    devices = lax.axis_size(("group", "patch"))
    halo_rows = HALO
    coarse_nodes = COARSE
    owners = coarse_owner[:, 0]
    gathered_index = owners * coarse_nodes + coarse_row
    node_range = jnp.arange(node_count, dtype=jnp.int32)
    padded_range = jnp.arange(node_count + 2 * halo_rows, dtype=jnp.int32)
    fine_onehot = (node_range[:, None] == fine_receiver[None, :]).astype(jnp.bfloat16)
    coarse_onehot = (node_range[:, None] == coarse_receiver[None, :]).astype(jnp.bfloat16)
    fine_to_receiver = (fine_receiver[:, None] == node_range[None, :]).astype(jnp.bfloat16)
    coarse_to_receiver = (coarse_receiver[:, None] == node_range[None, :]).astype(jnp.bfloat16)
    fine_to_sender = (fine_sender[:, None] == padded_range[None, :]).astype(jnp.bfloat16)
    gathered_range = jnp.arange(devices * coarse_nodes, dtype=jnp.int32)
    coarse_to_sender = (gathered_index[:, None] == gathered_range[None, :]).astype(jnp.bfloat16)
    latent = node_latent
    fine_state = fine_latent
    coarse_state = coarse_latent
    for layer_index in range(LAYERS):
        first = edge_first[layer_index]
        weight_edge = first[:width]
        weight_pair = first[width:]
        bias_row = edge_bias[layer_index]
        weight_second = edge_second[layer_index]
        gain_row = edge_gain[layer_index]
        padded = padded_2(latent, (("patch", 0),), halo_rows)
        own_coarse = latent[:coarse_nodes]
        sender_table = lax.all_gather(own_coarse, ("group", "patch"), axis=0, tiled=True)
        fine_ends = jnp.concatenate(
            [select_rows(fine_to_sender, padded), select_rows(fine_to_receiver, latent)], axis=1
        )
        coarse_ends = jnp.concatenate(
            [select_rows(coarse_to_sender, sender_table), select_rows(coarse_to_receiver, latent)],
            axis=1,
        )
        fine_state, fine_message = edge_block(
            fine_state, fine_ends, weight_edge, weight_pair, bias_row, weight_second, gain_row
        )
        coarse_state, coarse_message = edge_block(
            coarse_state, coarse_ends, weight_edge, weight_pair, bias_row, weight_second, gain_row
        )
        summed = jnp.dot(fine_onehot, fine_message, preferred_element_type=jnp.float32) + jnp.dot(
            coarse_onehot, coarse_message, preferred_element_type=jnp.float32
        )
        summed = summed.astype(jnp.bfloat16)
        node_weights = node_first[layer_index]
        pre = (
            jnp.dot(latent, node_weights[:width], preferred_element_type=jnp.float32)
            + jnp.dot(summed, node_weights[width:], preferred_element_type=jnp.float32)
            + node_bias[layer_index]
        )
        hidden = jax.nn.silu(pre).astype(jnp.bfloat16)
        output = jnp.dot(hidden, node_second[layer_index], preferred_element_type=jnp.float32)
        latent = (latent.astype(jnp.float32) + norm_rows(output, node_gain[layer_index])).astype(
            jnp.bfloat16
        )
    return (latent, fine_state, coarse_state)


def solution(mesh):
    in_specs = (
        P(("group", "patch"), None),
        P(("group", "patch"), None),
        P(("group", "patch"), None),
        P(("group", "patch")),
        P(("group", "patch")),
        P(("group", "patch"), None),
        P(("group", "patch")),
        P(("group", "patch")),
        P(),
        P(),
        P(),
        P(),
        P(),
        P(),
        P(),
        P(),
    )
    out_specs = (
        P(("group", "patch"), None),
        P(("group", "patch"), None),
        P(("group", "patch"), None),
    )
    return jax.shard_map(body, mesh=mesh, in_specs=in_specs, out_specs=out_specs, check_vma=False)
```

profile of v0, /device:TPU:1, one launch (start us, length us, event | category | flops | bytes accessed | tf_op | source)
XLA Modules:
  0.0 181.6 jit_solution(11054618840922823359)
XLA Ops:
  7.2 1.4 slice.125
  8.7 0.9 fusion.169
  9.6 2.2 %collective-permute-start = (bf16[64,512]{1,0:T(8,128)(2,1)S(1)}, bf16[64,512]{1,0:T(8,128)(2,1)S(1)}, u32[]{:S(2)}, u32[]{:S(2)}) collective-permute-start(bf16[64,512]{1,0:T(8,128)(2,1)S(1)} %get-tuple-element.8), channel_id=1, source_target_pairs={{0,1},{1,2},{2,3},{3,4},{4,5},{5,6},{6,7},{7,8},{8,9},{9,10},{10,1... | collective-permute-start | bytes 196616 | tf_op jit(solution)/shard_map/ppermute | solution.py:18
  11.8 3.7 %collective-permute-start.1 = (bf16[64,512]{1,0:T(8,128)(2,1)S(1)}, bf16[64,512]{1,0:T(8,128)(2,1)S(1)}, u32[]{:S(2)}, u32[]{:S(2)}) collective-permute-start(bf16[64,512]{1,0:T(8,128)(2,1)S(1)} %get-tuple-element.9), channel_id=1, source_target_pairs={{1,0},{2,1},{3,2},{4,3},{5,4},{6,5},{7,6},{8,7},{9,8},{10,9},{11,1... | collective-permute-start | bytes 196616 | tf_op jit(solution)/shard_map/ppermute | solution.py:21
  15.5 0.8 fusion.173
  16.2 0.8 fusion.172
  17.0 0.8 fusion.171
  17.8 2.3 %convolution_convert_fusion.1 = bf16[512,512]{1,0:T(8,128)(2,1)} fusion(bf16[320,512]{1,0:T(8,128)(2,1)} %param.16, s32[512]{0:T(512)} %param.23), kind=kOutput, calls=%fused_computation.55 | convolution fusion | flops 168198144 | bytes 854016 | tf_op jit(solution)/shard_map/dot_general | solution.py:34
  20.0 2.3 %fusion.106 = f32[320,512]{1,0:T(8,128)} fusion(bf16[320,512]{1,0:T(8,128)(2,1)} %param.16, bf16[2,1024,512]{2,1,0:T(8,128)(2,1)} %param.28), kind=kOutput, calls=%fused_computation.118 | convolution fusion | flops 167772160 | bytes 1507328 | tf_op jit(solution)/shard_map/dot_general | solution.py:113
  22.4 2.7 %fusion.102 = f32[512,512]{1,0:T(8,128)} fusion(bf16[512,512]{1,0:T(8,128)(2,1)} %param.18, bf16[2,1536,512]{2,1,0:T(8,128)(2,1)} %param.24), kind=kOutput, calls=%fused_computation.115 | convolution fusion | flops 268435456 | bytes 2097152 | tf_op jit(solution)/shard_map/dot_general | solution.py:39
  25.2 2.5 %fusion.18 = bf16[2048,512]{1,0:T(8,128)(2,1)} fusion(bf16[320,512]{1,0:T(8,128)(2,1)S(1)} %copy-done.7, s32[2048]{0:T(1024)S(1)} %copy-done.15), kind=kOutput, calls=%fused_computation.29 | convolution fusion | flops 672792576 | bytes 2433024 | tf_op jit(solution)/shard_map/dot_general | solution.py:34
  27.7 1.0 copy.20
  28.7 2.4 %copy.19 = bf16[2048,512]{0,1:T(8,128)(2,1)} copy(bf16[2048,512]{1,0:T(8,128)(2,1)S(1)} %copy-done.5) | data formatting | bytes 4194304 | tf_op args[1]
  31.2 1.7 fusion.16
  33.0 5.6 %fusion = f32[2048,512]{1,0:T(8,128)} fusion(bf16[2048,512]{1,0:T(8,128)(2,1)S(1)} %copy-done.19, bf16[2048,512]{1,0:T(8,128)(2,1)S(1)} %fusion.16, bf16[2,1536,512]{2,1,0:T(8,128)(2,1)} %param.24), kind=kOutput, calls=%fused_computation | convolution fusion | flops 2155872256 | bytes 9437184 | tf_op jit(solution)/shard_map/dot_general | solution.py:38
  38.6 7.1 %fusion.174 = (f32[2048]{0:T(1024)S(1)}, f32[2048,512]{0,1:T(8,128)}) fusion(bf16[2,512,512]{2,1,0:T(8,128)(2,1)S(1)} %copy-done.13, f32[2048,512]{1,0:T(8,128)} %fusion, bf16[2048,512]{1,0:T(8,128)(2,1)S(1)} %copy-done.5, f32[512]{0:T(512)S(1)} %bitcast.116, bf16[2,1536,512]{2,1,0:T(8,128)(2,1)} %param.24), kind=kOutput, calls=%fused_computation.187 | convolution fusion | flops 2155870208 | bytes 11544576 | tf_op jit(solution)/shard_map/dot_general | solution.py:41
  45.7 2.8 %multiply_reduce_fusion.1 = f32[2048]{0:T(1024)S(1)} fusion(f32[2048,512]{0,1:T(8,128)} %get-tuple-element.19, f32[2048]{0:T(1024)S(1)} %broadcast_multiply_fusion.1), kind=kLoop, calls=%fused_computation.17 | loop fusion | flops 3143680 | bytes 4210688 | tf_op jit(solution)/shard_map/reduce_sum | solution.py:29
  48.5 0.6 copy-done.1
  49.1 2.0 %fusion.21 = f32[320,512]{1,0:T(8,128)} fusion(f32[2048,512]{0,1:T(8,128)S(1)} %copy-done.1, f32[512]{0:T(512)S(1)} %bitcast.105, f32[2048]{0:T(1024)S(1)} %add_rsqrt_fusion.1, f32[2048]{0:T(1024)S(1)} %broadcast_multiply_fusion.1, s32[2048]{0:T(1024)S(1)} %copy-done.15), kind=kOutput, calls=%fused_computation.33 | convolution fusion | flops 675938304 | bytes 4876288 | tf_op jit(solution)/shard_map/dot_general | solution.py:107
  51.1 1.1 add_convert_fusion.1
  52.3 28.3 %all-gather.3.cloned.1.call-done = bf16[2048,512]{1,0:T(8,128)(2,1)} async-done(((bf16[16,512]{1,0:T(8,128)(2,1)}), bf16[2048,512]{1,0:T(8,128)(2,1)}) %all-gather.3.cloned.1.call-update) | async-done | bytes 2097168 | tf_op jit(solution)/shard_map/all_gather | solution.py:93
  80.6 3.7 %fusion.42 = bf16[512,512]{1,0:T(8,128)(2,1)} fusion(bf16[2048,512]{1,0:T(8,128)(2,1)} %all-gather.3.cloned.1.call-done, s32[512]{0:T(512)S(1)} %add.176), kind=kOutput, calls=%fused_computation.56 | convolution fusion | flops 1075052544 | bytes 2623488 | tf_op jit(solution)/shard_map/dot_general | solution.py:34
  84.3 3.3 %fusion.177 = (f32[512]{0:T(512)S(1)}, f32[512,512]{0,1:T(8,128)S(1)}) fusion(bf16[2,512,512]{2,1,0:T(8,128)(2,1)} %param.26, f32[512,512]{1,0:T(8,128)} %fusion.102, bf16[2,1536,512]{2,1,0:T(8,128)(2,1)} %param.24, bf16[512,512]{1,0:T(8,128)(2,1)} %convolution_convert_fusion.1, bf16[512,512]{1,0:T(8,128)(2,1)} %fusion.42, f32[512]{0:T(512)S(1)} %bitcast.117), kind=kOutput, calls=%fused_computation.188 | convolution fusion | flops 809500160 | bytes 4722688 | tf_op jit(solution)/shard_map/dot_general | solution.py:41
  87.8 2.4 %multiply_convert_fusion.5 = bf16[320,512]{1,0:T(8,128)(2,1)S(1)} fusion(f32[320,512]{1,0:T(8,128)} %fusion.106, f32[320,512]{1,0:T(8,128)} %fusion.21, f32[512,512]{0,1:T(8,128)S(1)} %get-tuple-element.21, bf16[2,1024,512]{2,1,0:T(8,128)(2,1)} %param.28, f32[512]{0:T(512)S(1)} %bitcast.107, f32[512]{0:T(512)S(1)} %add_rsqrt_fusion.5, ...), kind=kOutput, calls=%fused_computation.98 | convolution fusion | flops 338231296 | bytes 3221504 | tf_op jit(solution)/shard_map/dot_general | solution.py:114
  90.2 1.5 fusion.182
  91.9 1.2 add_convert_fusion.5
  93.1 0.6 slice.150
  93.7 2.5 %fusion.19 = bf16[2048,512]{1,0:T(8,128)(2,1)} fusion(bf16[320,512]{1,0:T(8,128)(2,1)S(1)} %add_convert_fusion.5, s32[2048]{0:T(1024)S(1)} %copy-done.15), kind=kOutput, calls=%fused_computation.30 | convolution fusion | flops 672792576 | bytes 2433024 | tf_op jit(solution)/shard_map/dot_general | solution.py:34
  96.2 1.3 add_convert_fusion.3
  97.5 2.5 %fusion.91 = f32[512,512]{1,0:T(8,128)} fusion(bf16[512,512]{0,1:T(8,128)(2,1)S(1)} %add_convert_fusion.3, bf16[2,1536,512]{2,1,0:T(8,128)(2,1)} %param.24), kind=kOutput, calls=%fused_computation.105 | convolution fusion | flops 268435456 | bytes 2097152 | tf_op jit(solution)/shard_map/dot_general | solution.py:39
  100.3 4.8 %collective-permute-start.3 = (bf16[64,512]{1,0:T(8,128)(2,1)S(1)}, bf16[64,512]{1,0:T(8,128)(2,1)S(1)}, u32[]{:S(2)}, u32[]{:S(2)}) collective-permute-start(bf16[64,512]{1,0:T(8,128)(2,1)S(1)} %get-tuple-element.7), channel_id=1, source_target_pairs={{1,0},{2,1},{3,2},{4,3},{5,4},{6,5},{7,6},{8,7},{9,8},{10,9},{11,1... | collective-permute-start | bytes 196616 | tf_op jit(solution)/shard_map/ppermute | solution.py:21
  105.1 2.2 %fusion.95 = f32[320,512]{1,0:T(8,128)} fusion(bf16[320,512]{1,0:T(8,128)(2,1)S(1)} %add_convert_fusion.5, bf16[2,1024,512]{2,1,0:T(8,128)(2,1)} %param.28), kind=kOutput, calls=%fused_computation.108 | convolution fusion | flops 167772160 | bytes 1507328 | tf_op jit(solution)/shard_map/dot_general | solution.py:113
  107.3 1.3 convolution_convert_fusion
  108.6 1.5 fusion.17
  110.2 5.5 %fusion.4 = f32[2048,512]{1,0:T(8,128)} fusion(bf16[2048,512]{1,0:T(8,128)(2,1)S(1)} %copy-done.18, bf16[2048,512]{1,0:T(8,128)(2,1)S(1)} %fusion.17, bf16[2,1536,512]{2,1,0:T(8,128)(2,1)} %param.24), kind=kOutput, calls=%fused_computation.4 | convolution fusion | flops 2155872256 | bytes 9437184 | tf_op jit(solution)/shard_map/dot_general | solution.py:38
  115.7 7.4 %fusion.183 = (f32[2048]{0:T(1024)S(1)}, f32[2048,512]{0,1:T(8,128)}) fusion(bf16[2,512,512]{2,1,0:T(8,128)(2,1)} %param.26, f32[2048,512]{1,0:T(8,128)} %fusion.4, bf16[2048,512]{0,1:T(8,128)(2,1)S(1)} %add_convert_fusion.1, f32[512]{0:T(512)S(1)} %bitcast.113, bf16[2,1536,512]{2,1,0:T(8,128)(2,1)} %param.24), kind=kOutput, calls=%fused_computation.190 | convolution fusion | flops 2155870208 | bytes 11544576 | tf_op jit(solution)/shard_map/dot_general | solution.py:41
  123.1 2.8 %multiply_reduce_fusion = f32[2048]{0:T(1024)S(1)} fusion(f32[2048,512]{0,1:T(8,128)} %get-tuple-element.25, f32[2048]{0:T(1024)S(1)} %broadcast_multiply_fusion), kind=kLoop, calls=%fused_computation.10 | loop fusion | flops 3143680 | bytes 4210688 | tf_op jit(solution)/shard_map/reduce_sum | solution.py:29
  125.9 0.6 copy-done
  126.5 2.4 %add_convert_fusion = bf16[2048,512]{0,1:T(8,128)(2,1)} fusion(bf16[2048,512]{0,1:T(8,128)(2,1)S(1)} %add_convert_fusion.1, f32[2048,512]{0,1:T(8,128)S(1)} %copy-done, f32[512]{0:T(512)S(1)} %bitcast.101, f32[2048]{0:T(1024)S(1)} %add_rsqrt_fusion, f32[2048]{0:T(1024)S(1)} %broadcast_multiply_fusion), kind=kLoop, calls=%fused_computation.8 | loop fusion | flops 6291456 | bytes 8407040 | tf_op jit(solution)/shard_map/convert_element_type | solution.py:43
  128.9 3.9 %copy.21 = bf16[2048,512]{1,0:T(8,128)(2,1)} copy(bf16[2048,512]{0,1:T(8,128)(2,1)} %add_convert_fusion) | data formatting | bytes 4194304
  132.9 4.1 %fusion.20 = f32[320,512]{1,0:T(8,128)} fusion(f32[2048,512]{0,1:T(8,128)} %get-tuple-element.25, f32[512]{0:T(512)S(1)} %bitcast.102, f32[2048]{0:T(1024)S(1)} %add_rsqrt_fusion, f32[2048]{0:T(1024)S(1)} %broadcast_multiply_fusion, s32[2048]{0:T(1024)S(1)} %copy-done.15), kind=kOutput, calls=%fused_computation.32 | convolution fusion | flops 675938304 | bytes 4876288 | tf_op jit(solution)/shard_map/dot_general | solution.py:107
  137.0 25.9 %all-gather.5.cloned.1.call-done = bf16[2048,512]{1,0:T(8,128)(2,1)} async-done(((bf16[16,512]{1,0:T(8,128)(2,1)}), bf16[2048,512]{1,0:T(8,128)(2,1)}) %all-gather.5.cloned.1.call-update) | async-done | bytes 2097168 | tf_op jit(solution)/shard_map/all_gather | solution.py:93
  163.0 3.7 %fusion.43 = bf16[512,512]{1,0:T(8,128)(2,1)} fusion(bf16[2048,512]{1,0:T(8,128)(2,1)} %all-gather.5.cloned.1.call-done, s32[512]{0:T(512)S(1)} %add.176), kind=kOutput, calls=%fused_computation.57 | convolution fusion | flops 1075052544 | bytes 2623488 | tf_op jit(solution)/shard_map/dot_general | solution.py:34
  166.6 2.8 %fusion.186 = (f32[512]{0:T(512)S(1)}, f32[512,512]{0,1:T(8,128)S(1)}) fusion(bf16[2,512,512]{2,1,0:T(8,128)(2,1)} %param.26, f32[512,512]{1,0:T(8,128)S(1)} %copy-done.9, bf16[2,1536,512]{2,1,0:T(8,128)(2,1)} %param.24, bf16[512,512]{1,0:T(8,128)(2,1)S(1)} %copy-done.17, bf16[512,512]{1,0:T(8,128)(2,1)} %fusion.43, f32[512]{0:T(512)S(1)} %bitcast.114), kind=kOutput, calls=%fused_computation.191 | convolution fusion | flops 809500160 | bytes 4722688 | tf_op jit(solution)/shard_map/dot_general | solution.py:41
  169.9 1.0 copy.22
  170.9 2.2 %multiply_convert_fusion.4 = bf16[320,512]{1,0:T(8,128)(2,1)S(1)} fusion(f32[320,512]{1,0:T(8,128)} %fusion.95, f32[320,512]{1,0:T(8,128)} %fusion.20, f32[512,512]{0,1:T(8,128)S(1)} %get-tuple-element.27, bf16[2,1024,512]{2,1,0:T(8,128)(2,1)} %param.28, f32[512]{0:T(512)S(1)} %bitcast.104, f32[512]{0:T(512)S(1)} %add_rsqrt_fusion.3, ...), kind=kOutput, calls=%fused_computation.95 | convolution fusion | flops 338231296 | bytes 3221504 | tf_op jit(solution)/shard_map/dot_general | solution.py:114
  173.1 0.4 fusion.191
  173.8 0.9 add_convert_fusion.4
  (68 shorter events, 1.7 us)
Async XLA Ops:
  7.2 18.0 %copy-start.7 = (bf16[320,512]{1,0:T(8,128)(2,1)S(1)}, bf16[320,512]{1,0:T(8,128)(2,1)}, u32[]{:S(2)}) copy-start(bf16[320,512]{1,0:T(8,128)(2,1)} %param.16) | copy-start | bytes 983044
  7.2 17.9 %copy-start.10 = (f32[2,512]{1,0:T(2,128)S(1)}, f32[2,512]{1,0:T(2,128)}, u32[]{:S(2)}) copy-start(f32[2,512]{1,0:T(2,128)} %param.31) | copy-start | bytes 12292
  7.2 18.0 %copy-start.15 = (s32[2048]{0:T(1024)S(1)}, s32[2048]{0:T(1024)}, u32[]{:S(2)}) copy-start(s32[2048]{0:T(1024)} %param.20) | copy-start | bytes 24580
  7.2 73.4 %all-gather.3.cloned.1.call-start = ((), (), s32[]{:S(2)}) async-start(), calls=%async_computation | async-start | bytes 2113536 | tf_op jit(solution)/shard_map/all_gather | solution.py:93
  8.6 154.3 %all-gather.5.cloned.1.call-start = ((), (), s32[]{:S(2)}) async-start(), calls=%async_computation.1 | async-start | bytes 2113536 | tf_op jit(solution)/shard_map/all_gather | solution.py:93
  9.6 21.6 %collective-permute-start = (bf16[64,512]{1,0:T(8,128)(2,1)S(1)}, bf16[64,512]{1,0:T(8,128)(2,1)S(1)}, u32[]{:S(2)}, u32[]{:S(2)}) collective-permute-start(bf16[64,512]{1,0:T(8,128)(2,1)S(1)} %get-tuple-element.8), channel_id=1, source_target_pairs={{0,1},{1,2},{2,3},{3,4},{4,5},{5,6},{6,7},{7,8},{8,9},{9,10},{10,1... | collective-permute-start | bytes 196616 | tf_op jit(solution)/shard_map/ppermute | solution.py:18
  11.8 19.4 %collective-permute-start.1 = (bf16[64,512]{1,0:T(8,128)(2,1)S(1)}, bf16[64,512]{1,0:T(8,128)(2,1)S(1)}, u32[]{:S(2)}, u32[]{:S(2)}) collective-permute-start(bf16[64,512]{1,0:T(8,128)(2,1)S(1)} %get-tuple-element.9), channel_id=1, source_target_pairs={{1,0},{2,1},{3,2},{4,3},{5,4},{6,5},{7,6},{8,7},{9,8},{10,9},{11,1... | collective-permute-start | bytes 196616 | tf_op jit(solution)/shard_map/ppermute | solution.py:21
  22.4 5.3 %copy-start.12 = (s32[512,1]{0,1:T(1,128)S(1)}, s32[512,1]{0,1:T(1,128)}, u32[]{:S(2)}) copy-start(s32[512,1]{0,1:T(1,128)} %param.21) | copy-start | bytes 6148
  22.4 5.3 %copy-start.6 = (bf16[512,512]{1,0:T(8,128)(2,1)S(1)}, bf16[512,512]{1,0:T(8,128)(2,1)}, u32[]{:S(2)}) copy-start(bf16[512,512]{1,0:T(8,128)(2,1)} %param.18) | copy-start | bytes 1572868
  25.1 3.6 %copy-start.5 = (bf16[2048,512]{1,0:T(8,128)(2,1)S(1)}, bf16[2048,512]{1,0:T(8,128)(2,1)}, u32[]{:S(2)}) copy-start(bf16[2048,512]{1,0:T(8,128)(2,1)} %param.17) | copy-start | bytes 6291460
  27.7 3.5 %copy-start.11 = (s32[512]{0:T(512)S(1)}, s32[512]{0:T(512)}, u32[]{:S(2)}) copy-start(s32[512]{0:T(512)} %param.22) | copy-start | bytes 6148
  27.7 3.5 %copy-start.14 = (s32[2048]{0:T(1024)S(1)}, s32[2048]{0:T(1024)}, u32[]{:S(2)}) copy-start(s32[2048]{0:T(1024)} %param.19) | copy-start | bytes 24580
  31.1 1.8 copy-start.19
  32.9 5.6 %copy-start.13 = (bf16[2,512,512]{2,1,0:T(8,128)(2,1)S(1)}, bf16[2,512,512]{2,1,0:T(8,128)(2,1)}, u32[]{:S(2)}) copy-start(bf16[2,512,512]{2,1,0:T(8,128)(2,1)} %param.26) | copy-start | bytes 3145732
  45.7 3.4 %copy-start.1 = (f32[2048,512]{0,1:T(8,128)S(1)}, f32[2048,512]{0,1:T(8,128)}, u32[]{:S(2)}) copy-start(f32[2048,512]{0,1:T(8,128)} %get-tuple-element.19) | copy-start | bytes 12582916
  48.5 2.6 %copy-start.2 = (bf16[2048,512]{0,1:T(8,128)(2,1)S(1)}, bf16[2048,512]{0,1:T(8,128)(2,1)}, u32[]{:S(2)}) copy-start(bf16[2048,512]{0,1:T(8,128)(2,1)} %copy.19) | copy-start | bytes 6291460
  84.3 3.5 %copy-start.16 = (s32[512]{0:T(512)S(1)}, s32[512]{0:T(512)}, u32[]{:S(2)}) copy-start(s32[512]{0:T(512)} %param.23) | copy-start | bytes 6148
  87.6 4.3 %copy-start.3 = (f32[512,512]{0,1:T(8,128)}, f32[512,512]{0,1:T(8,128)S(1)}, u32[]{:S(2)}) copy-start(f32[512,512]{0,1:T(8,128)S(1)} %get-tuple-element.21) | copy-start | bytes 3145732
  93.7 2.5 %copy-start.4 = (f32[512,512]{0,1:T(8,128)S(1)}, f32[512,512]{0,1:T(8,128)}, u32[]{:S(2)}) copy-start(f32[512,512]{0,1:T(8,128)} %copy-done.3) | copy-start | bytes 3145732
  100.0 8.6 %collective-permute-start.2 = (bf16[64,512]{1,0:T(8,128)(2,1)S(1)}, bf16[64,512]{1,0:T(8,128)(2,1)S(1)}, u32[]{:S(2)}, u32[]{:S(2)}) collective-permute-start(bf16[64,512]{1,0:T(8,128)(2,1)S(1)} %get-tuple-element.6), channel_id=1, source_target_pairs={{0,1},{1,2},{2,3},{3,4},{4,5},{5,6},{6,7},{7,8},{8,9},{9,10},{10,1... | collective-permute-start | bytes 196616 | tf_op jit(solution)/shard_map/ppermute | solution.py:18
  100.3 8.3 %collective-permute-start.3 = (bf16[64,512]{1,0:T(8,128)(2,1)S(1)}, bf16[64,512]{1,0:T(8,128)(2,1)S(1)}, u32[]{:S(2)}, u32[]{:S(2)}) collective-permute-start(bf16[64,512]{1,0:T(8,128)(2,1)S(1)} %get-tuple-element.7), channel_id=1, source_target_pairs={{1,0},{2,1},{3,2},{4,3},{5,4},{6,5},{7,6},{8,7},{9,8},{10,9},{11,1... | collective-permute-start | bytes 196616 | tf_op jit(solution)/shard_map/ppermute | solution.py:21
  107.3 2.8 %copy-start.18 = (bf16[2048,512]{1,0:T(8,128)(2,1)S(1)}, bf16[2048,512]{1,0:T(8,128)(2,1)}, u32[]{:S(2)}) copy-start(bf16[2048,512]{1,0:T(8,128)(2,1)} %fusion.19) | copy-start | bytes 6291460
  123.1 3.4 %copy-start = (f32[2048,512]{0,1:T(8,128)S(1)}, f32[2048,512]{0,1:T(8,128)}, u32[]{:S(2)}) copy-start(f32[2048,512]{0,1:T(8,128)} %get-tuple-element.25) | copy-start | bytes 12582916
  137.0 29.6 %copy-start.9 = (f32[512,512]{1,0:T(8,128)S(1)}, f32[512,512]{1,0:T(8,128)}, u32[]{:S(2)}) copy-start(f32[512,512]{1,0:T(8,128)} %fusion.91) | copy-start | bytes 3145732
  137.0 29.6 %copy-start.17 = (bf16[512,512]{1,0:T(8,128)(2,1)S(1)}, bf16[512,512]{1,0:T(8,128)(2,1)}, u32[]{:S(2)}) copy-start(bf16[512,512]{1,0:T(8,128)(2,1)} %convolution_convert_fusion) | copy-start | bytes 1572868
  169.9 3.2 %copy-start.8 = (bf16[2,512,512]{2,1,0:T(8,128)(2,1)S(1)}, bf16[2,512,512]{2,1,0:T(8,128)(2,1)}, u32[]{:S(2)}) copy-start(bf16[2,512,512]{2,1,0:T(8,128)(2,1)} %param.30) | copy-start | bytes 3145732
Sparse Core Ops, SparseCore 0:
  11.6 68.9 all-gather.2
  100.1 62.7 all-gather.4
where the time goes:
time: 182 us
  matrix products  73.3 us (40%)
  waiting for transfers between devices  54.3 us (30%)
  local copies, waits for them, and re-layouts  14.9 us (8%)
  between operations  14.3 us (8%)
  other arithmetic  13.7 us (8%)
  starting transfers between devices  11 us (6%)
    all_gather x2, waiting for transfers between devices, body(): lax.all_gather(own_coarse, ('group', 'patch'), axis=0, tiled=True)  54.3 us
    dot_general x4, matrix products, edge_block(): output = jnp.dot(hidden, weight_second, preferred_element_type=jnp.float32)  20.6 us
    dot_general x8, matrix products, select_rows(): jnp.dot(selector, table, preferred_element_type=jnp.float32)  19.2 us
    dot_general x2, matrix products, edge_block(): jnp.dot(endpoints, weight_pair, preferred_element_type=jnp.float32)  11.1 us
    unnamed x44, local copies, waits for them, and re-layouts  9.72 us
    ppermute x2, starting transfers between devices, padded_2(): lax.ppermute(lax.slice_in_dim(block, 0, width, axis=dim), axis, backward)  8.49 us
    reduce_sum x6, other arithmetic, norm_rows(): variance = jnp.mean(centred * centred, axis=-1, keepdims=True)  6.42 us
    dot_general x2, matrix products, body(): jnp.dot(fine_onehot, fine_message, preferred_element_type=jnp.float32)  6.12 us
  transfers between devices with their start and end apart: 6, of which 2 were waited for; matrix products, arithmetic and copies ran while one was open for 38% of the time, Pallas kernels for 0%

commit v1 on v0

--- a/solution.py
+++ b/solution.py
@@ -90,7 +90,18 @@
         gain_row = edge_gain[layer_index]
         padded = padded_2(latent, (("patch", 0),), halo_rows)
         own_coarse = latent[:coarse_nodes]
-        sender_table = lax.all_gather(own_coarse, ("group", "patch"), axis=0, tiled=True)
+        sender_table = jnp.concatenate(
+            jax.lax.all_to_all(
+                jnp.stack(
+                    tuple((own_coarse for _ in range(jax.lax.axis_size(("group", "patch"))))),
+                    axis=0,
+                ),
+                axis_name=("group", "patch"),
+                split_axis=0,
+                concat_axis=0,
+            ),
+            axis=0,
+        )
         fine_ends = jnp.concatenate(
             [select_rows(fine_to_sender, padded), select_rows(fine_to_receiver, latent)], axis=1
         )

time: 182 us -> 129 us (0.71)
  waiting for transfers between devices: 54.3 us -> 0.94 us
  starting transfers between devices: 11 us -> 26.3 us
  between operations: 14.3 us -> 1.04 us
  other arithmetic: 13.7 us -> 11.7 us
    all_gather x2 -> x0, waiting for transfers between devices: 54.3 us -> none  [body(): lax.all_gather(own_coarse, ('group', 'patch'), axis=0, tiled=True)]
    all_to_all x0 -> x2, starting transfers between devices: none -> 15.6 us  [body(): jax.lax.all_to_all(jnp.stack(tuple((own_coarse for _ in range(jax.lax.axi...]
    another operation x0 -> x2, local copies, waits for them, and re-layouts: none -> 3.18 us  [body(): jnp.stack(tuple((own_coarse for _ in range(jax.lax.axis_size(('group', 'p...]
    unnamed x44 -> x50, local copies, waits for them, and re-layouts: 9.72 us -> 9.76 us
  transfers between devices with their start and end apart: 6 -> 6, of which waited for: 2 -> 1; matrix products, arithmetic and copies ran while one was open for 38% -> 51% of each run, Pallas kernels for 0% -> 0%
where the time goes in v1:
time: 129 us; the launch traced here: 128 us
  matrix products  73.1 us (57%)
  starting transfers between devices  26.3 us (20%)
  local copies, waits for them, and re-layouts  14.7 us (11%)
  other arithmetic  11.7 us (9%)
    dot_general x4, matrix products, edge_block(): output = jnp.dot(hidden, weight_second, preferred_element_type=jnp.float32)  20.7 us
    dot_general x8, matrix products, select_rows(): jnp.dot(selector, table, preferred_element_type=jnp.float32)  18.3 us
    all_to_all x2, starting transfers between devices, body(): jax.lax.all_to_all(jnp.stack(tuple((own_coarse for _ in range(jax.lax.axi...  15.6 us
    dot_general x2, matrix products, edge_block(): jnp.dot(endpoints, weight_pair, preferred_element_type=jnp.float32)  11.1 us
    unnamed x50, local copies, waits for them, and re-layouts  9.76 us
    ppermute x2, starting transfers between devices, padded_2(): lax.ppermute(lax.slice_in_dim(block, 0, width, axis=dim), axis, backward)  7.15 us
    reduce_sum x6, other arithmetic, norm_rows(): variance = jnp.mean(centred * centred, axis=-1, keepdims=True)  6.42 us
    dot_general x2, matrix products, body(): jnp.dot(fine_onehot, fine_message, preferred_element_type=jnp.float32)  6.11 us
  transfers between devices with their start and end apart: 6, of which 1 were waited for; matrix products, arithmetic and copies ran while one was open for 51% of the time, Pallas kernels for 0%

profile of v1, /device:TPU:1, one launch (start us, length us, event | category | flops | bytes accessed | tf_op | source)
XLA Modules:
  0.0 127.7 jit_solution(3328317710258392440)
XLA Ops:
  0.7 1.0 fusion.169
  1.7 2.2 %collective-permute-start = (bf16[64,512]{1,0:T(8,128)(2,1)S(1)}, bf16[64,512]{1,0:T(8,128)(2,1)S(1)}, u32[]{:S(2)}, u32[]{:S(2)}) collective-permute-start(bf16[64,512]{1,0:T(8,128)(2,1)S(1)} %get-tuple-element.8), channel_id=1, source_target_pairs={{0,1},{1,2},{2,3},{3,4},{4,5},{5,6},{6,7},{7,8},{8,9},{9,10},{10,1... | collective-permute-start | bytes 196616 | tf_op jit(solution)/shard_map/ppermute | solution.py:18
  3.9 3.7 %collective-permute-start.1 = (bf16[64,512]{1,0:T(8,128)(2,1)S(1)}, bf16[64,512]{1,0:T(8,128)(2,1)S(1)}, u32[]{:S(2)}, u32[]{:S(2)}) collective-permute-start(bf16[64,512]{1,0:T(8,128)(2,1)S(1)} %get-tuple-element.9), channel_id=1, source_target_pairs={{1,0},{2,1},{3,2},{4,3},{5,4},{6,5},{7,6},{8,7},{9,8},{10,9},{11,1... | collective-permute-start | bytes 196616 | tf_op jit(solution)/shard_map/ppermute | solution.py:21
  7.6 0.7 slice.125
  8.3 1.6 %stack.4 = bf16[128,16,512]{2,1,0:T(8,128)(2,1)} broadcast(bf16[16,512]{1,0:T(8,128)(2,1)S(1)} %slice.125), dimensions={1,2} | broadcast | bytes 2113536 | tf_op jit(solution)/shard_map/stack | solution.py:95
  9.9 8.1 %all-to-all-start = ((bf16[128,16,512]{2,1,0:T(8,128)(2,1)}), bf16[128,16,512]{2,1,0:T(8,128)(2,1)}, u32[]{:S(2)}, u32[]{:S(2)}) async-start(bf16[128,16,512]{2,1,0:T(8,128)(2,1)} %stack.4), calls=%async_computation | async-start | bytes 4194304 | tf_op jit(solution)/shard_map/all_to_all | solution.py:94
  18.1 1.3 %convolution_convert_fusion.1 = bf16[512,512]{1,0:T(8,128)(2,1)} fusion(bf16[320,512]{1,0:T(8,128)(2,1)S(1)} %copy-done.8, s32[512]{0:T(512)S(1)} %copy-done.19), kind=kOutput, calls=%fused_computation.55 | convolution fusion | flops 168198144 | bytes 854016 | tf_op jit(solution)/shard_map/dot_general | solution.py:34
  19.4 2.3 %fusion.106 = f32[320,512]{1,0:T(8,128)} fusion(bf16[320,512]{1,0:T(8,128)(2,1)S(1)} %copy-done.8, bf16[2,1024,512]{2,1,0:T(8,128)(2,1)} %param.28), kind=kOutput, calls=%fused_computation.118 | convolution fusion | flops 167772160 | bytes 1507328 | tf_op jit(solution)/shard_map/dot_general | solution.py:124
  21.7 2.5 %fusion.18 = bf16[2048,512]{1,0:T(8,128)(2,1)} fusion(bf16[320,512]{1,0:T(8,128)(2,1)S(1)} %copy-done.8, s32[2048]{0:T(1024)S(1)} %copy-done.18), kind=kOutput, calls=%fused_computation.29 | convolution fusion | flops 672792576 | bytes 2433024 | tf_op jit(solution)/shard_map/dot_general | solution.py:34
  24.3 2.5 %fusion.102 = f32[512,512]{1,0:T(8,128)} fusion(bf16[512,512]{1,0:T(8,128)(2,1)S(1)} %copy-done.7, bf16[2,1536,512]{2,1,0:T(8,128)(2,1)} %param.24), kind=kOutput, calls=%fused_computation.115 | convolution fusion | flops 268435456 | bytes 2097152 | tf_op jit(solution)/shard_map/dot_general | solution.py:39
  26.8 1.0 copy.20
  27.8 2.4 %copy.19 = bf16[2048,512]{0,1:T(8,128)(2,1)} copy(bf16[2048,512]{1,0:T(8,128)(2,1)S(1)} %copy-done.6) | data formatting | bytes 4194304 | tf_op args[1]
  30.3 1.7 %fusion.16 = bf16[2048,512]{1,0:T(8,128)(2,1)S(1)} fusion(s32[2048]{0:T(1024)S(1)} %copy-done.17, bf16[64,512]{1,0:T(8,128)(2,1)S(1)} %collective-permute-done.1, bf16[320,512]{1,0:T(8,128)(2,1)S(1)} %copy-done.8, bf16[64,512]{1,0:T(8,128)(2,1)S(1)} %collective-permute-done), kind=kOutput, calls=%fused_computation.27 | convolution fusion | flops 942866432 | bytes 2564096 | tf_op jit(solution)/shard_map/dot_general | solution.py:34
  32.0 5.5 %fusion = f32[2048,512]{1,0:T(8,128)} fusion(bf16[2048,512]{1,0:T(8,128)(2,1)S(1)} %copy-done.22, bf16[2048,512]{1,0:T(8,128)(2,1)S(1)} %fusion.16, bf16[2,1536,512]{2,1,0:T(8,128)(2,1)} %param.24), kind=kOutput, calls=%fused_computation | convolution fusion | flops 2155872256 | bytes 9437184 | tf_op jit(solution)/shard_map/dot_general | solution.py:38
  37.5 7.3 %fusion.174 = (f32[2048]{0:T(1024)S(1)}, f32[2048,512]{0,1:T(8,128)}) fusion(bf16[2,512,512]{2,1,0:T(8,128)(2,1)} %param.26, f32[2048,512]{1,0:T(8,128)} %fusion, bf16[2048,512]{1,0:T(8,128)(2,1)S(1)} %copy-done.6, f32[512]{0:T(512)S(1)} %bitcast.118, bf16[2,1536,512]{2,1,0:T(8,128)(2,1)} %param.24), kind=kOutput, calls=%fused_computation.187 | convolution fusion | flops 2155870208 | bytes 11544576 | tf_op jit(solution)/shard_map/dot_general | solution.py:41
  44.8 2.8 %multiply_reduce_fusion.1 = f32[2048]{0:T(1024)S(1)} fusion(f32[2048,512]{0,1:T(8,128)} %get-tuple-element.19, f32[2048]{0:T(1024)S(1)} %broadcast_multiply_fusion.1), kind=kLoop, calls=%fused_computation.17 | loop fusion | flops 3143680 | bytes 4210688 | tf_op jit(solution)/shard_map/reduce_sum | solution.py:29
  47.6 0.6 copy-done.1
  48.2 2.0 %fusion.21 = f32[320,512]{1,0:T(8,128)} fusion(f32[2048,512]{0,1:T(8,128)S(1)} %copy-done.1, f32[512]{0:T(512)S(1)} %bitcast.107, f32[2048]{0:T(1024)S(1)} %add_rsqrt_fusion.1, f32[2048]{0:T(1024)S(1)} %broadcast_multiply_fusion.1, s32[2048]{0:T(1024)S(1)} %copy-done.18), kind=kOutput, calls=%fused_computation.33 | convolution fusion | flops 675938304 | bytes 4876288 | tf_op jit(solution)/shard_map/dot_general | solution.py:118
  50.2 1.1 add_convert_fusion.1
  51.4 3.7 %fusion.42 = bf16[512,512]{1,0:T(8,128)(2,1)} fusion(bf16[2048,512]{1,0:T(8,128)(2,1)} %bitcast.7, s32[512]{0:T(512)S(1)} %add.176), kind=kOutput, calls=%fused_computation.56 | convolution fusion | flops 1075052544 | bytes 2623488 | tf_op jit(solution)/shard_map/dot_general | solution.py:34
  55.1 3.3 %fusion.177 = (f32[512]{0:T(512)S(1)}, f32[512,512]{0,1:T(8,128)S(1)}) fusion(bf16[2,512,512]{2,1,0:T(8,128)(2,1)} %param.26, f32[512,512]{1,0:T(8,128)} %fusion.102, bf16[2,1536,512]{2,1,0:T(8,128)(2,1)} %param.24, bf16[512,512]{1,0:T(8,128)(2,1)} %convolution_convert_fusion.1, bf16[512,512]{1,0:T(8,128)(2,1)} %fusion.42, f32[512]{0:T(512)S(1)} %bitcast.119), kind=kOutput, calls=%fused_computation.188 | convolution fusion | flops 809500160 | bytes 4722688 | tf_op jit(solution)/shard_map/dot_general | solution.py:41
  58.6 3.1 %multiply_convert_fusion.5 = bf16[320,512]{1,0:T(8,128)(2,1)} fusion(f32[320,512]{1,0:T(8,128)} %fusion.106, f32[320,512]{1,0:T(8,128)} %fusion.21, f32[512,512]{0,1:T(8,128)S(1)} %get-tuple-element.21, bf16[2,1024,512]{2,1,0:T(8,128)(2,1)} %param.28, f32[512]{0:T(512)S(1)} %bitcast.109, f32[512]{0:T(512)S(1)} %add_rsqrt_fusion.5, ...), kind=kOutput, calls=%fused_computation.98 | convolution fusion | flops 338231296 | bytes 3221504 | tf_op jit(solution)/shard_map/dot_general | solution.py:125
  61.7 1.6 %fusion.182 = (f32[320]{0:T(512)S(1)}, f32[320,512]{1,0:T(8,128)S(1)}) fusion(bf16[320,512]{1,0:T(8,128)(2,1)} %multiply_convert_fusion.5, bf16[2,512,512]{2,1,0:T(8,128)(2,1)} %param.30), kind=kOutput, calls=%fused_computation.189 | convolution fusion | flops 167935680 | bytes 1508608 | tf_op jit(solution)/shard_map/dot_general | solution.py:129
  63.3 0.2 multiply_reduce_fusion.5
  63.8 2.3 %fusion.95 = f32[320,512]{1,0:T(8,128)} fusion(bf16[320,512]{1,0:T(8,128)(2,1)S(1)} %add_convert_fusion.5, bf16[2,1024,512]{2,1,0:T(8,128)(2,1)} %param.28), kind=kOutput, calls=%fused_computation.108 | convolution fusion | flops 167772160 | bytes 1507328 | tf_op jit(solution)/shard_map/dot_general | solution.py:124
  66.1 2.5 %fusion.19 = bf16[2048,512]{1,0:T(8,128)(2,1)} fusion(bf16[320,512]{1,0:T(8,128)(2,1)S(1)} %add_convert_fusion.5, s32[2048]{0:T(1024)S(1)} %copy-done.18), kind=kOutput, calls=%fused_computation.30 | convolution fusion | flops 672792576 | bytes 2433024 | tf_op jit(solution)/shard_map/dot_general | solution.py:34
  68.8 2.5 %fusion.91 = f32[512,512]{1,0:T(8,128)} fusion(bf16[512,512]{0,1:T(8,128)(2,1)S(1)} %add_convert_fusion.3, bf16[2,1536,512]{2,1,0:T(8,128)(2,1)} %param.24), kind=kOutput, calls=%fused_computation.105 | convolution fusion | flops 268435456 | bytes 2097152 | tf_op jit(solution)/shard_map/dot_general | solution.py:39
  71.4 1.3 %collective-permute-start.2 = (bf16[64,512]{1,0:T(8,128)(2,1)S(1)}, bf16[64,512]{1,0:T(8,128)(2,1)S(1)}, u32[]{:S(2)}, u32[]{:S(2)}) collective-permute-start(bf16[64,512]{1,0:T(8,128)(2,1)S(1)} %get-tuple-element.6), channel_id=1, source_target_pairs={{0,1},{1,2},{2,3},{3,4},{4,5},{5,6},{6,7},{7,8},{8,9},{9,10},{10,1... | collective-permute-start | bytes 196616 | tf_op jit(solution)/shard_map/ppermute | solution.py:18
  72.7 3.4 %collective-permute-start.3 = (bf16[64,512]{1,0:T(8,128)(2,1)S(1)}, bf16[64,512]{1,0:T(8,128)(2,1)S(1)}, u32[]{:S(2)}, u32[]{:S(2)}) collective-permute-start(bf16[64,512]{1,0:T(8,128)(2,1)S(1)} %get-tuple-element.7), channel_id=1, source_target_pairs={{1,0},{2,1},{3,2},{4,3},{5,4},{6,5},{7,6},{8,7},{9,8},{10,9},{11,1... | collective-permute-start | bytes 196616 | tf_op jit(solution)/shard_map/ppermute | solution.py:21
  76.2 1.3 convolution_convert_fusion
  77.4 1.6 %stack.5 = bf16[128,16,512]{2,1,0:T(8,128)(2,1)} broadcast(bf16[16,512]{1,0:T(8,128)(2,1)S(1)} %slice.150), dimensions={1,2} | broadcast | bytes 2113536 | tf_op jit(solution)/shard_map/stack | solution.py:95
  79.0 7.4 %all-to-all-start.1 = ((bf16[128,16,512]{2,1,0:T(8,128)(2,1)}), bf16[128,16,512]{2,1,0:T(8,128)(2,1)}, u32[]{:S(2)}, u32[]{:S(2)}) async-start(bf16[128,16,512]{2,1,0:T(8,128)(2,1)} %stack.5), calls=%async_computation.1 | async-start | bytes 4194304 | tf_op jit(solution)/shard_map/all_to_all | solution.py:94
  86.5 1.5 %fusion.17 = bf16[2048,512]{1,0:T(8,128)(2,1)S(1)} fusion(s32[2048]{0:T(1024)S(1)} %copy-done.17, bf16[64,512]{1,0:T(8,128)(2,1)S(1)} %collective-permute-done.3, bf16[320,512]{1,0:T(8,128)(2,1)S(1)} %add_convert_fusion.5, bf16[64,512]{1,0:T(8,128)(2,1)S(1)} %collective-permute-done.2), kind=kOutput, calls=%fused_computation.28 | convolution fusion | flops 942866432 | bytes 2564096 | tf_op jit(solution)/shard_map/dot_general | solution.py:34
  88.1 5.6 %fusion.4 = f32[2048,512]{1,0:T(8,128)} fusion(bf16[2048,512]{1,0:T(8,128)(2,1)S(1)} %copy-done.21, bf16[2048,512]{1,0:T(8,128)(2,1)S(1)} %fusion.17, bf16[2,1536,512]{2,1,0:T(8,128)(2,1)} %param.24), kind=kOutput, calls=%fused_computation.4 | convolution fusion | flops 2155872256 | bytes 9437184 | tf_op jit(solution)/shard_map/dot_general | solution.py:38
  93.6 7.3 %fusion.183 = (f32[2048]{0:T(1024)S(1)}, f32[2048,512]{0,1:T(8,128)}) fusion(bf16[2,512,512]{2,1,0:T(8,128)(2,1)} %param.26, f32[2048,512]{1,0:T(8,128)} %fusion.4, bf16[2048,512]{0,1:T(8,128)(2,1)S(1)} %add_convert_fusion.1, f32[512]{0:T(512)S(1)} %bitcast.115, bf16[2,1536,512]{2,1,0:T(8,128)(2,1)} %param.24), kind=kOutput, calls=%fused_computation.190 | convolution fusion | flops 2155870208 | bytes 11544576 | tf_op jit(solution)/shard_map/dot_general | solution.py:41
  101.0 2.8 %multiply_reduce_fusion = f32[2048]{0:T(1024)S(1)} fusion(f32[2048,512]{0,1:T(8,128)} %get-tuple-element.25, f32[2048]{0:T(1024)S(1)} %broadcast_multiply_fusion), kind=kLoop, calls=%fused_computation.10 | loop fusion | flops 3143680 | bytes 4210688 | tf_op jit(solution)/shard_map/reduce_sum | solution.py:29
  103.8 0.6 copy-done
  104.4 2.5 %add_convert_fusion = bf16[2048,512]{0,1:T(8,128)(2,1)} fusion(bf16[2048,512]{0,1:T(8,128)(2,1)S(1)} %add_convert_fusion.1, f32[2048,512]{0,1:T(8,128)S(1)} %copy-done, f32[512]{0:T(512)S(1)} %bitcast.103, f32[2048]{0:T(1024)S(1)} %add_rsqrt_fusion, f32[2048]{0:T(1024)S(1)} %broadcast_multiply_fusion), kind=kLoop, calls=%fused_computation.8 | loop fusion | flops 6291456 | bytes 8407040 | tf_op jit(solution)/shard_map/convert_element_type | solution.py:43
  106.9 3.9 %copy.21 = bf16[2048,512]{1,0:T(8,128)(2,1)} copy(bf16[2048,512]{0,1:T(8,128)(2,1)} %add_convert_fusion) | data formatting | bytes 4194304
  110.8 4.1 %fusion.20 = f32[320,512]{1,0:T(8,128)} fusion(f32[2048,512]{0,1:T(8,128)} %get-tuple-element.25, f32[512]{0:T(512)S(1)} %bitcast.104, f32[2048]{0:T(1024)S(1)} %add_rsqrt_fusion, f32[2048]{0:T(1024)S(1)} %broadcast_multiply_fusion, s32[2048]{0:T(1024)S(1)} %copy-done.18), kind=kOutput, calls=%fused_computation.32 | convolution fusion | flops 675938304 | bytes 4876288 | tf_op jit(solution)/shard_map/dot_general | solution.py:118
  114.9 0.9 all-to-all-done.1
  115.9 3.7 %fusion.43 = bf16[512,512]{1,0:T(8,128)(2,1)} fusion(bf16[2048,512]{1,0:T(8,128)(2,1)} %bitcast.18, s32[512]{0:T(512)S(1)} %add.176), kind=kOutput, calls=%fused_computation.57 | convolution fusion | flops 1075052544 | bytes 2623488 | tf_op jit(solution)/shard_map/dot_general | solution.py:34
  119.6 2.8 %fusion.186 = (f32[512]{0:T(512)S(1)}, f32[512,512]{0,1:T(8,128)S(1)}) fusion(bf16[2,512,512]{2,1,0:T(8,128)(2,1)} %param.26, f32[512,512]{1,0:T(8,128)S(1)} %copy-done.10, bf16[2,1536,512]{2,1,0:T(8,128)(2,1)} %param.24, bf16[512,512]{1,0:T(8,128)(2,1)S(1)} %copy-done.20, bf16[512,512]{1,0:T(8,128)(2,1)} %fusion.43, f32[512]{0:T(512)S(1)} %bitcast.116), kind=kOutput, calls=%fused_computation.191 | convolution fusion | flops 809500160 | bytes 4722688 | tf_op jit(solution)/shard_map/dot_general | solution.py:41
  122.8 1.0 copy.22
  123.8 2.2 %multiply_convert_fusion.4 = bf16[320,512]{1,0:T(8,128)(2,1)S(1)} fusion(f32[320,512]{1,0:T(8,128)} %fusion.95, f32[320,512]{1,0:T(8,128)} %fusion.20, f32[512,512]{0,1:T(8,128)S(1)} %get-tuple-element.27, bf16[2,1024,512]{2,1,0:T(8,128)(2,1)} %param.28, f32[512]{0:T(512)S(1)} %bitcast.106, f32[512]{0:T(512)S(1)} %add_rsqrt_fusion.3, ...), kind=kOutput, calls=%fused_computation.95 | convolution fusion | flops 338231296 | bytes 3221504 | tf_op jit(solution)/shard_map/dot_general | solution.py:125
  126.0 0.4 fusion.191
  126.5 0.2 multiply_reduce_fusion.4
  126.7 0.9 add_convert_fusion.4
  (74 shorter events, 1.2 us)
Async XLA Ops:
  0.6 17.5 %copy-start.8 = (bf16[320,512]{1,0:T(8,128)(2,1)S(1)}, bf16[320,512]{1,0:T(8,128)(2,1)}, u32[]{:S(2)}) copy-start(bf16[320,512]{1,0:T(8,128)(2,1)} %param.16) | copy-start | bytes 983044
  0.6 17.4 %copy-start.11 = (f32[2,512]{1,0:T(2,128)S(1)}, f32[2,512]{1,0:T(2,128)}, u32[]{:S(2)}) copy-start(f32[2,512]{1,0:T(2,128)} %param.25) | copy-start | bytes 12292
  0.7 17.4 %copy-start.12 = (f32[2,512]{1,0:T(2,128)S(1)}, f32[2,512]{1,0:T(2,128)}, u32[]{:S(2)}) copy-start(f32[2,512]{1,0:T(2,128)} %param.27) | copy-start | bytes 12292
  0.7 17.4 %copy-start.13 = (f32[2,512]{1,0:T(2,128)S(1)}, f32[2,512]{1,0:T(2,128)}, u32[]{:S(2)}) copy-start(f32[2,512]{1,0:T(2,128)} %param.29) | copy-start | bytes 12292
  0.7 17.4 %copy-start.14 = (f32[2,512]{1,0:T(2,128)S(1)}, f32[2,512]{1,0:T(2,128)}, u32[]{:S(2)}) copy-start(f32[2,512]{1,0:T(2,128)} %param.31) | copy-start | bytes 12292
  0.7 17.5 %copy-start.19 = (s32[512]{0:T(512)S(1)}, s32[512]{0:T(512)}, u32[]{:S(2)}) copy-start(s32[512]{0:T(512)} %param.23) | copy-start | bytes 6148
  1.7 28.6 %collective-permute-start = (bf16[64,512]{1,0:T(8,128)(2,1)S(1)}, bf16[64,512]{1,0:T(8,128)(2,1)S(1)}, u32[]{:S(2)}, u32[]{:S(2)}) collective-permute-start(bf16[64,512]{1,0:T(8,128)(2,1)S(1)} %get-tuple-element.8), channel_id=1, source_target_pairs={{0,1},{1,2},{2,3},{3,4},{4,5},{5,6},{6,7},{7,8},{8,9},{9,10},{10,1... | collective-permute-start | bytes 196616 | tf_op jit(solution)/shard_map/ppermute | solution.py:18
  3.9 26.4 %collective-permute-start.1 = (bf16[64,512]{1,0:T(8,128)(2,1)S(1)}, bf16[64,512]{1,0:T(8,128)(2,1)S(1)}, u32[]{:S(2)}, u32[]{:S(2)}) collective-permute-start(bf16[64,512]{1,0:T(8,128)(2,1)S(1)} %get-tuple-element.9), channel_id=1, source_target_pairs={{1,0},{2,1},{3,2},{4,3},{5,4},{6,5},{7,6},{8,7},{9,8},{10,9},{11,1... | collective-permute-start | bytes 196616 | tf_op jit(solution)/shard_map/ppermute | solution.py:21
  8.3 13.4 %copy-start.18 = (s32[2048]{0:T(1024)S(1)}, s32[2048]{0:T(1024)}, u32[]{:S(2)}) copy-start(s32[2048]{0:T(1024)} %param.20) | copy-start | bytes 24580
  9.9 41.5 %all-to-all-start = ((bf16[128,16,512]{2,1,0:T(8,128)(2,1)}), bf16[128,16,512]{2,1,0:T(8,128)(2,1)}, u32[]{:S(2)}, u32[]{:S(2)}) async-start(bf16[128,16,512]{2,1,0:T(8,128)(2,1)} %stack.4), calls=%async_computation | async-start | bytes 4194304 | tf_op jit(solution)/shard_map/all_to_all | solution.py:94
  19.4 4.8 %copy-start.7 = (bf16[512,512]{1,0:T(8,128)(2,1)S(1)}, bf16[512,512]{1,0:T(8,128)(2,1)}, u32[]{:S(2)}) copy-start(bf16[512,512]{1,0:T(8,128)(2,1)} %param.18) | copy-start | bytes 1572868
  21.7 5.0 %copy-start.16 = (s32[512,1]{0,1:T(1,128)S(1)}, s32[512,1]{0,1:T(1,128)}, u32[]{:S(2)}) copy-start(s32[512,1]{0,1:T(1,128)} %param.21) | copy-start | bytes 6148
  21.7 6.1 %copy-start.6 = (bf16[2048,512]{1,0:T(8,128)(2,1)S(1)}, bf16[2048,512]{1,0:T(8,128)(2,1)}, u32[]{:S(2)}) copy-start(bf16[2048,512]{1,0:T(8,128)(2,1)} %param.17) | copy-start | bytes 6291460
  24.2 6.0 %copy-start.15 = (s32[512]{0:T(512)S(1)}, s32[512]{0:T(512)}, u32[]{:S(2)}) copy-start(s32[512]{0:T(512)} %param.22) | copy-start | bytes 6148
  24.3 6.0 %copy-start.17 = (s32[2048]{0:T(1024)S(1)}, s32[2048]{0:T(1024)}, u32[]{:S(2)}) copy-start(s32[2048]{0:T(1024)} %param.19) | copy-start | bytes 24580
  30.2 1.8 %copy-start.22 = (bf16[2048,512]{1,0:T(8,128)(2,1)S(1)}, bf16[2048,512]{1,0:T(8,128)(2,1)}, u32[]{:S(2)}) copy-start(bf16[2048,512]{1,0:T(8,128)(2,1)} %fusion.18) | copy-start | bytes 6291460
  44.8 3.4 %copy-start.1 = (f32[2048,512]{0,1:T(8,128)S(1)}, f32[2048,512]{0,1:T(8,128)}, u32[]{:S(2)}) copy-start(f32[2048,512]{0,1:T(8,128)} %get-tuple-element.19) | copy-start | bytes 12582916
  47.6 2.6 %copy-start.2 = (bf16[2048,512]{0,1:T(8,128)(2,1)S(1)}, bf16[2048,512]{0,1:T(8,128)(2,1)}, u32[]{:S(2)}) copy-start(bf16[2048,512]{0,1:T(8,128)(2,1)} %copy.19) | copy-start | bytes 6291460
  58.4 5.2 %copy-start.3 = (f32[512,512]{0,1:T(8,128)}, f32[512,512]{0,1:T(8,128)S(1)}, u32[]{:S(2)}) copy-start(f32[512,512]{0,1:T(8,128)S(1)} %get-tuple-element.21) | copy-start | bytes 3145732
  63.7 4.9 %copy-start.4 = (f32[512,512]{0,1:T(8,128)S(1)}, f32[512,512]{0,1:T(8,128)}, u32[]{:S(2)}) copy-start(f32[512,512]{0,1:T(8,128)} %copy-done.3) | copy-start | bytes 3145732
  63.7 4.9 %copy-start.5 = (bf16[512,512]{0,1:T(8,128)(2,1)S(1)}, bf16[512,512]{0,1:T(8,128)(2,1)}, u32[]{:S(2)}) copy-start(bf16[512,512]{0,1:T(8,128)(2,1)} %copy.20) | copy-start | bytes 1572868
  71.4 15.1 %collective-permute-start.2 = (bf16[64,512]{1,0:T(8,128)(2,1)S(1)}, bf16[64,512]{1,0:T(8,128)(2,1)S(1)}, u32[]{:S(2)}, u32[]{:S(2)}) collective-permute-start(bf16[64,512]{1,0:T(8,128)(2,1)S(1)} %get-tuple-element.6), channel_id=1, source_target_pairs={{0,1},{1,2},{2,3},{3,4},{4,5},{5,6},{6,7},{7,8},{8,9},{9,10},{10,1... | collective-permute-start | bytes 196616 | tf_op jit(solution)/shard_map/ppermute | solution.py:18
  72.7 13.8 %collective-permute-start.3 = (bf16[64,512]{1,0:T(8,128)(2,1)S(1)}, bf16[64,512]{1,0:T(8,128)(2,1)S(1)}, u32[]{:S(2)}, u32[]{:S(2)}) collective-permute-start(bf16[64,512]{1,0:T(8,128)(2,1)S(1)} %get-tuple-element.7), channel_id=1, source_target_pairs={{1,0},{2,1},{3,2},{4,3},{5,4},{6,5},{7,6},{8,7},{9,8},{10,9},{11,1... | collective-permute-start | bytes 196616 | tf_op jit(solution)/shard_map/ppermute | solution.py:21
  79.0 36.8 %all-to-all-start.1 = ((bf16[128,16,512]{2,1,0:T(8,128)(2,1)}), bf16[128,16,512]{2,1,0:T(8,128)(2,1)}, u32[]{:S(2)}, u32[]{:S(2)}) async-start(bf16[128,16,512]{2,1,0:T(8,128)(2,1)} %stack.5), calls=%async_computation.1 | async-start | bytes 4194304 | tf_op jit(solution)/shard_map/all_to_all | solution.py:94
  86.5 1.6 %copy-start.21 = (bf16[2048,512]{1,0:T(8,128)(2,1)S(1)}, bf16[2048,512]{1,0:T(8,128)(2,1)}, u32[]{:S(2)}) copy-start(bf16[2048,512]{1,0:T(8,128)(2,1)} %fusion.19) | copy-start | bytes 6291460
  101.0 3.4 %copy-start = (f32[2048,512]{0,1:T(8,128)S(1)}, f32[2048,512]{0,1:T(8,128)}, u32[]{:S(2)}) copy-start(f32[2048,512]{0,1:T(8,128)} %get-tuple-element.25) | copy-start | bytes 12582916
  114.9 4.6 %copy-start.10 = (f32[512,512]{1,0:T(8,128)S(1)}, f32[512,512]{1,0:T(8,128)}, u32[]{:S(2)}) copy-start(f32[512,512]{1,0:T(8,128)} %fusion.91) | copy-start | bytes 3145732
  114.9 4.6 %copy-start.20 = (bf16[512,512]{1,0:T(8,128)(2,1)S(1)}, bf16[512,512]{1,0:T(8,128)(2,1)}, u32[]{:S(2)}) copy-start(bf16[512,512]{1,0:T(8,128)(2,1)} %convolution_convert_fusion) | copy-start | bytes 1572868
  122.8 3.2 %copy-start.9 = (bf16[2,512,512]{2,1,0:T(8,128)(2,1)S(1)}, bf16[2,512,512]{2,1,0:T(8,128)(2,1)}, u32[]{:S(2)}) copy-start(bf16[2,512,512]{2,1,0:T(8,128)(2,1)} %param.30) | copy-start | bytes 3145732
